TPU v7x, 1024 devices: a whole 4x4x32 slice. The times are simulated.
1024 devices in a mesh: tm: 128 (over z_lo, y, x), head: 8 (over z_hi, core).
Axes of the slice: x: 4, y: 4, z: 32 (z_hi: 4, z_lo: 8; z = z_hi * 8 + z_lo), core: 2. Of those that a mesh axis runs over, the one named last changes fastest.
Arguments:
- query_rows: bfloat16 [32768, 4096], P('tm', 'head'), may hold values from -6 to 6
- key_rows: bfloat16 [32768, 4096], P('tm', 'head'), may hold values from -6 to 6
- value_rows: bfloat16 [32768, 4096], P('tm', 'head'), may hold values from -12 to 12
- frame_counts: int32 [128], replicated, may hold values from 1 to 4, 384 in all
- history: bfloat16 [256, 4096], P('tm', 'head'), may hold values from -3 to 3
- offsets: int32 [128, 128], P('tm'), may hold values from 0 to 127, each once within a row
- cotangent: bfloat16 [65536, 2048], P('tm'), may hold values from -0.09375 to 0.09375
Outputs:
- attended: bfloat16 [32768, 4096], P('tm', 'head')
- disc_grad: float32 [2048, 4096], P('tm', 'head')
Inputs may be any that keep to these rules, and one draw needn't show every extreme that they name: Each row of offsets names every number below 128 once.
All inputs are finite; a program needn't handle non-finite values.
Results may differ from a plain program's by a relative error of at most 0.0049.
Values may be sent and summed in bfloat16 or wider, within the bound.
A program may use at most 32 MiB of HBM per device.

v0:
```python
import math

import jax
import jax.numpy as jnp
from jax import lax
from jax.sharding import PartitionSpec as P

HD = 128
TPF = 64
WINB = 4


def from_behind(x, axis, by):
    devices = lax.axis_size(axis)
    pairs = [(i, i + by) for i in range(devices) if 0 <= i + by < devices]
    return lax.ppermute(x, axis, pairs)


def body(query_rows, key_rows, value_rows, frame_counts, history, offsets, cotangent):
    tok_rows, feat_width = query_rows.shape
    local_heads = feat_width // HD
    block_total = lax.axis_size("tm")
    own_block = lax.axis_index("tm")
    score_scale = 1.0 / math.sqrt(HD)
    key_value = jnp.stack([key_rows, value_rows])
    pieces = []
    for distance in range(WINB - 1, 0, -1):
        pieces.append(from_behind(key_value, "tm", distance))
    window = jnp.concatenate(pieces + [key_value], axis=1)
    source_block = own_block - (WINB - 1) + jnp.arange(WINB, dtype=jnp.int32)
    block_match = jnp.arange(block_total, dtype=jnp.int32)[None, :] == source_block[:, None]
    block_count = jnp.sum(jnp.where(block_match, frame_counts[None, :], 0), axis=1)
    frame_index = jnp.arange(tok_rows, dtype=jnp.int32) // TPF
    kept_mask = (
        (source_block[:, None] >= 0) & (frame_index[None, :] < block_count[:, None])
    ).reshape(WINB * tok_rows)
    key_window = window[0].reshape(WINB * tok_rows, local_heads, HD)
    value_window = window[1].reshape(WINB * tok_rows, local_heads, HD)
    query_heads = query_rows.reshape(tok_rows, local_heads, HD)
    scores = (
        jnp.einsum("qhd,khd->hqk", query_heads, key_window, preferred_element_type=jnp.float32)
        * score_scale
    )
    scores = jnp.where(kept_mask[None, None, :], scores, -jnp.inf)
    row_max = jnp.max(scores, axis=-1, keepdims=True)
    weights = jnp.exp(scores - row_max)
    probs = (weights / jnp.sum(weights, axis=-1, keepdims=True)).astype(jnp.bfloat16)
    mixed = jnp.einsum("hqk,khd->qhd", probs, value_window, preferred_element_type=jnp.float32)
    attended = mixed.astype(jnp.bfloat16).reshape(tok_rows, feat_width)
    tile_rows = history.shape[0]
    source_tile = (own_block - offsets[0]) % block_total
    source_row = (
        source_tile[:, None] * tile_rows + jnp.arange(tile_rows, dtype=jnp.int32)[None, :]
    ).reshape(-1)
    incoming = lax.all_gather(history, "tm", axis=0, tiled=True)
    piece_rows = incoming.shape[0]
    selector = (source_row[:, None] == jnp.arange(piece_rows, dtype=jnp.int32)[None, :]).astype(
        jnp.bfloat16
    )
    clip_hist = jnp.dot(selector, incoming, preferred_element_type=jnp.float32).astype(jnp.bfloat16)
    disc_clip = jnp.concatenate([clip_hist, attended], axis=0)
    disc_grad = lax.psum_scatter(
        lax.dot_general(
            cotangent, disc_clip, (((0,), (0,)), ((), ())), preferred_element_type=jnp.float32
        ),
        "tm",
        scatter_dimension=0,
        tiled=True,
    )
    return (attended, disc_grad)


def solution(mesh):
    in_specs = (
        P("tm", "head"),
        P("tm", "head"),
        P("tm", "head"),
        P(),
        P("tm", "head"),
        P("tm", None),
        P("tm", None),
    )
    out_specs = (P("tm", "head"), P("tm", "head"))
    return jax.shard_map(body, mesh=mesh, in_specs=in_specs, out_specs=out_specs, check_vma=False)
```

profile of v0, /device:TPU:256, one launch (start us, length us, event | category | flops | bytes accessed | tf_op | source)
XLA Modules:
  0.0 1638.5 jit_solution(4650997451079598636)
XLA Ops:
  7.2 0.0 copy-start
  7.2 0.0 reduce-scatter.4.cloned.1.call-start
  7.2 1.2 copy.29
  8.5 1.1 copy.30
  9.5 0.8 pad_maximum_fusion
  10.4 4.2 collective-permute-start.2
  14.6 4.7 collective-permute-start.1
  19.2 4.4 collective-permute-start
  23.6 0.7 fusion.27
  24.3 0.8 select_reduce_fusion
  25.1 0.1 compare_and_fusion
  25.2 0.1 iota_add_fusion
  25.3 0.1 add.57
  25.4 521.8 %all-gather = bf16[128,2,512]{2,1,0:T(2,128)(2,1)S(1)} all-gather(bf16[1,2,512]{2,1,0:T(2,128)(2,1)} %bitcast.57), channel_id=1, replica_groups=mesh['tm'=128,'head'=8] {'tm'}, dimensions={0}, use_global_device_ids=true | all-gather | bytes 264192 | tf_op jit(solution)/shard_map/all_gather | solution.py:55
  547.3 0.1 reshape.94
  547.4 0.3 convolution_convert_fusion
  547.7 0.0 collective-permute-done.2
  547.7 0.0 collective-permute-done.1
  547.7 0.0 collective-permute-done
  547.7 1.5 maximum_maximum_fusion
  549.2 1.1 fusion.32
  550.4 4.7 fusion.33
  555.1 3.3 fusion.9
  558.5 1.1 copy.35
  559.5 0.0 copy-done
  559.6 0.0 copy-start.1
  559.6 3.2 convolution_bitcast_fusion
  562.8 5.3 copy.39
  568.1 0.0 copy-done.1
  568.1 0.0 reduce-scatter.4.cloned.1.call-update
  568.1 1063.5 %reduce-scatter.4.cloned.1.call-done = f32[16,512]{1,0:T(8,128)} async-done(((f32[2048,512]{1,0:T(8,128)}), f32[16,512]{1,0:T(8,128)}) %reduce-scatter.4.cloned.1.call-update) | async-done | bytes 32784
  (4 shorter events, 0.0 us)
Async XLA Ops:
  7.2 552.4 %copy-start = (bf16[512,2048]{1,0:T(8,128)(2,1)S(1)}, bf16[512,2048]{1,0:T(8,128)(2,1)}, u32[]{:S(2)}) copy-start(bf16[512,2048]{1,0:T(8,128)(2,1)} %param.13) | copy-start | bytes 6291460
  7.2 1624.4 %reduce-scatter.4.cloned.1.call-start = ((), (), s32[]{:S(2)}) async-start(), calls=%async_computation.1 | async-start | bytes 4227072
  10.4 537.3 %collective-permute-start.2 = (bf16[2,256,512]{1,2,0:T(8,128)(2,1)}, bf16[2,256,512]{1,2,0:T(8,128)(2,1)}, u32[]{:S(2)}, u32[]{:S(2)}) collective-permute-start(bf16[2,256,512]{1,2,0:T(8,128)(2,1)} %pad_maximum_fusion), channel_id=1, source_target_pairs={{0,8},{8,16},{16,24},{24,32},{32,40},{40,48},{48,56},{56,64},{64,7... | collective-permute-start | bytes 1572872 | tf_op jit(solution)/shard_map/ppermute | solution.py:16
  14.6 533.1 %collective-permute-start.1 = (bf16[2,256,512]{1,2,0:T(8,128)(2,1)}, bf16[2,256,512]{1,2,0:T(8,128)(2,1)}, u32[]{:S(2)}, u32[]{:S(2)}) collective-permute-start(bf16[2,256,512]{1,2,0:T(8,128)(2,1)} %pad_maximum_fusion), channel_id=1, source_target_pairs={{0,16},{8,24},{16,32},{24,40},{32,48},{40,56},{48,64},{56,72},{64,... | collective-permute-start | bytes 1572872 | tf_op jit(solution)/shard_map/ppermute | solution.py:16
  19.2 528.4 %collective-permute-start = (bf16[2,256,512]{1,2,0:T(8,128)(2,1)}, bf16[2,256,512]{1,2,0:T(8,128)(2,1)}, u32[]{:S(2)}, u32[]{:S(2)}) collective-permute-start(bf16[2,256,512]{1,2,0:T(8,128)(2,1)} %pad_maximum_fusion), channel_id=1, source_target_pairs={{0,24},{8,32},{16,40},{24,48},{32,56},{40,64},{48,72},{56,80},{64,... | collective-permute-start | bytes 1572872 | tf_op jit(solution)/shard_map/ppermute | solution.py:16
  559.6 8.6 copy-start.1
Sparse Core Ops, SparseCore 0:
  568.3 1063.3 reduce-scatter.3
where the time goes:
time: 1640 us
  waiting for transfers between devices  1060 us (65%)
  blocking collectives  522 us (32%)
    unnamed x2, waiting for transfers between devices  1060 us
    all_gather x1, blocking collectives, body(): incoming = lax.all_gather(history, 'tm', axis=0, tiled=True)  522 us
  transfers between devices with their start and end apart: 4, of which 1 were waited for; matrix products, arithmetic and copies ran while one was open for 0% of the time, Pallas kernels for 0%

commit v1 on v0

v1 whole, which is shorter than its diff:
```python
import math

import jax
import jax.numpy as jnp
from jax import lax
from jax.experimental import pallas as pl
from jax.experimental.pallas import tpu as pltpu
from jax.sharding import PartitionSpec as P

HD = 128
TPF = 64
WINB = 4
NX = 4
NY = 4
MESH = pl.DeviceIdType.MESH
F32 = jnp.float32
BF16 = jnp.bfloat16


def remote(src, dst, send, recv, target):
    return pltpu.make_async_remote_copy(
        src_ref=src,
        dst_ref=dst,
        send_sem=send,
        recv_sem=recv,
        device_id={"tm": target},
        device_id_type=MESH,
    )


def make_kernel(blocks, tok, feat, tiles, outs):
    nz = blocks // (NX * NY)
    half = feat // 2
    halves = (slice(0, half), slice(half, feat))
    heads = feat // HD
    rows = outs // blocks
    plane = outs // NX
    scale = 1.0 / math.sqrt(HD)

    def kernel(
        counts, query_hbm, key_hbm, value_hbm, history, offsets, cot_hbm,
        attended_ref, grad_ref,
        query, keys, values, cot, cot_t, clip, hist_all, hist_f32,
        send1, recv1, own1, send2, recv2, own2, send3, recv3, own3,
        local_sem, kv_send, kv_recv, ag_send, ag_recv,
        send1_sem, recv1_sem, send2_sem, recv2_sem, send3_sem, recv3_sem,
    ):
        me = lax.axis_index("tm")
        x = lax.rem(me, NX)
        y = lax.rem(me // NX, NY)
        z = me // (NX * NY)

        def at_x(k):
            return me - x + lax.rem(x + k, NX)

        def at_y(k):
            return me + (lax.rem(y + k, NY) - y) * NX

        def at_z(k):
            return me + (lax.rem(z + k, nz) - z) * (NX * NY)

        peers = [at_x(k) for k in range(1, NX)]
        peers += [at_y(k) for k in range(1, NY)]
        peers += [at_z(k) for k in range(1, nz)]

        local = [
            pltpu.make_async_copy(cot_hbm, cot, local_sem.at[0]),
            pltpu.make_async_copy(query_hbm, query, local_sem.at[1]),
            pltpu.make_async_copy(key_hbm, keys.at[WINB - 1], local_sem.at[2]),
            pltpu.make_async_copy(value_hbm, values.at[WINB - 1], local_sem.at[3]),
            pltpu.make_async_copy(history, hist_all.at[me], local_sem.at[4]),
        ]
        for copy in local:
            copy.start()

        barrier = pltpu.get_barrier_semaphore()
        for peer in peers:
            pl.semaphore_signal(barrier, inc=1, device_id={"tm": peer}, device_id_type=MESH)
        for distance in range(1, WINB):
            @pl.when(me >= distance)
            def _():
                pl.semaphore_signal(
                    barrier, inc=1, device_id={"tm": me - distance}, device_id_type=MESH
                )

            @pl.when(me + distance < blocks)
            def _():
                pl.semaphore_signal(
                    barrier, inc=1, device_id={"tm": me + distance}, device_id_type=MESH
                )
        around = jnp.minimum(me, WINB - 1) + jnp.minimum(blocks - 1 - me, WINB - 1)
        pl.semaphore_wait(barrier, len(peers) + around)

        kv = [[], []]
        for part in range(2):
            for distance in range(1, WINB):
                target = lax.rem(me + distance, blocks)
                for which, (src, dst) in enumerate(((key_hbm, keys), (value_hbm, values))):
                    i = (part * (WINB - 1) + distance - 1) * 2 + which
                    copy = remote(
                        src.at[:, halves[part]],
                        dst.at[WINB - 1 - distance, :, halves[part]],
                        kv_send.at[i],
                        kv_recv.at[i],
                        target,
                    )
                    kv[part].append((distance, copy))

        def start_kv(part):
            for distance, copy in kv[part]:
                @pl.when(me + distance < blocks)
                def _():
                    copy.start()

        def wait_kv(part):
            for distance, copy in kv[part]:
                @pl.when(me >= distance)
                def _():
                    copy.wait_recv()

        def gather(first, width, slot, targets):
            block = hist_all.at[pl.ds(first, width)]
            copies = []
            for i, target in enumerate(targets):
                copies.append(
                    remote(block, block, ag_send.at[slot + i], ag_recv.at[slot + i], target)
                )
            return copies

        gather_x = gather(me, 1, 0, [at_x(k) for k in range(1, NX)])
        gather_y = gather(me - x, NX, 3, [at_y(k) for k in range(1, NY)])
        gather_z = gather(z * NX * NY, NX * NY, 6, [at_z(k) for k in range(1, nz)])

        local[4].wait()
        for copy in gather_x:
            copy.start()
        start_kv(0)
        start_kv(1)

        for distance in range(1, WINB):
            @pl.when(me < distance)
            def _():
                keys[WINB - 1 - distance] = jnp.zeros((tok, feat), BF16)
                values[WINB - 1 - distance] = jnp.zeros((tok, feat), BF16)

        local[0].wait()

        def turn(c, _):
            block = cot[:, pl.ds(pl.multiple_of(c * 128, 128), 128)].T
            for e in range(128 // (NX * rows)):
                zy = c * (128 // (NX * rows)) + e
                for to_x in range(NX):
                    first = (e * NX + to_x) * rows
                    cot_t[to_x, lax.rem(zy, NY), zy // NY] = block[first : first + rows]
            return 0

        lax.fori_loop(0, outs // 256, turn, 0)
        for copy in gather_x:
            copy.wait_recv()
        for copy in gather_y:
            copy.start()
        lax.fori_loop(outs // 256, outs // 128, turn, 0)
        for copy in gather_y:
            copy.wait_recv()
        for copy in gather_z:
            copy.start()

        kept = []
        frame = lax.broadcasted_iota(jnp.int32, (1, tok), 1) // TPF
        for slot in range(WINB):
            source = me - (WINB - 1) + slot
            count = jnp.where(source >= 0, counts[jnp.maximum(source, 0)], 0)
            kept.append(frame < count)
        kept = jnp.concatenate(kept, axis=1)

        clip_rows = 2 * blocks
        tile = jnp.bitwise_and(me - offsets[...], blocks - 1).astype(F32).astype(BF16)
        spread = (
            lax.broadcasted_iota(jnp.int32, (blocks, clip_rows), 1) // tiles
            == lax.broadcasted_iota(jnp.int32, (blocks, clip_rows), 0)
        )
        spread = jnp.where(spread, 1.0, 0.0).astype(BF16)
        source_tile = jnp.dot(
            jnp.broadcast_to(tile, (16, blocks)), spread, preferred_element_type=F32
        )[0:1]
        hist_row = lax.broadcasted_iota(jnp.int32, (clip_rows, clip_rows), 0)
        clip_row = lax.broadcasted_iota(jnp.int32, (clip_rows, clip_rows), 1)
        chosen = (lax.rem(hist_row, blocks).astype(F32) == source_tile) & (
            hist_row // blocks == lax.rem(clip_row, tiles)
        )
        chosen = jnp.where(chosen, 1.0, 0.0).astype(BF16)

        for copy in gather_z:
            copy.wait_recv()
        hist_f32[...] = hist_all[...].astype(F32)
        pieces = []
        for t in range(tiles):
            line = [hist_f32[:, t * heads + c, :] for c in range(heads)]
            pieces.append(jnp.concatenate(line, axis=1))
        hist_rows = jnp.concatenate(pieces, axis=0).astype(BF16)
        clip[0:clip_rows] = lax.dot_general(
            chosen, hist_rows, (((0,), (0,)), ((), ())), preferred_element_type=F32
        ).astype(BF16)

        def attend(head):
            columns = slice(head * HD, (head + 1) * HD)
            key_head = keys[:, :, columns].reshape(WINB * tok, HD)
            value_head = values[:, :, columns].reshape(WINB * tok, HD)
            scores = lax.dot_general(
                query[:, columns], key_head, (((1,), (1,)), ((), ())), preferred_element_type=F32
            )
            scores = jnp.where(kept, scores * scale, -jnp.inf)
            weights = jnp.exp(scores - jnp.max(scores, axis=1, keepdims=True))
            probs = weights * (1.0 / jnp.sum(weights, axis=1, keepdims=True))
            mixed = jnp.dot(probs.astype(BF16), value_head, preferred_element_type=F32)
            clip[clip_rows : clip_rows + tok, columns] = mixed.astype(BF16)

        def product(part, to):
            left = cot_t[to] if part == 0 else cot_t[:, to]
            return jnp.dot(
                left.reshape(plane, clip_rows + tok),
                clip[:, halves[part]],
                preferred_element_type=F32,
            )

        place = (x, y)
        reach = (at_x, at_y)
        first_copies, second_copies, third_copies = [[], []], [[], []], [[], []]
        local[1].wait()
        local[2].wait()
        local[3].wait()
        for part in range(2):
            wait_kv(part)
            for head in range(part * heads // 2, (part + 1) * heads // 2):
                attend(head)
            for k in range(1, 4):
                send1[part, k - 1] = (
                    product(part, lax.rem(place[part] + k, 4)).astype(BF16).reshape(send1.shape[2:])
                )
                copy = remote(
                    send1.at[part, k - 1],
                    recv1.at[part, k - 1],
                    send1_sem.at[part, k - 1],
                    recv1_sem.at[part, k - 1],
                    reach[part](k),
                )
                copy.start()
                first_copies[part].append(copy)
            own1[part] = product(part, place[part]).reshape(own1.shape[1:])
        write_back = pltpu.make_async_copy(
            clip.at[clip_rows : clip_rows + tok], attended_ref, local_sem.at[5]
        )
        write_back.start()

        for part in range(2):
            for copy in first_copies[part]:
                copy.wait_recv()
            other = 1 - part

            def total1(to):
                total = own1[part, to]
                for k in range(3):
                    total += recv1[part, k, to].astype(F32)
                return total

            for k in range(1, 4):
                send2[part, k - 1] = total1(lax.rem(place[other] + k, 4)).astype(BF16)
                copy = remote(
                    send2.at[part, k - 1],
                    recv2.at[part, k - 1],
                    send2_sem.at[part, k - 1],
                    recv2_sem.at[part, k - 1],
                    reach[other](k),
                )
                copy.start()
                second_copies[part].append(copy)
            own2[part] = total1(place[other])

        for part in range(2):
            for copy in second_copies[part]:
                copy.wait_recv()
            total = own2[part]
            for k in range(3):
                total += recv2[part, k].astype(F32)
            own3[part] = total
            for k in range(1, nz):
                send3[part, k - 1] = own3[part, lax.rem(z + k, nz)].astype(BF16)
                copy = remote(
                    send3.at[part, k - 1],
                    recv3.at[part, k - 1],
                    send3_sem.at[part, k - 1],
                    recv3_sem.at[part, k - 1],
                    at_z(k),
                )
                copy.start()
                third_copies[part].append(copy)

        for part in range(2):
            for copy in third_copies[part]:
                copy.wait_recv()
            total = own3[part, z]
            for k in range(nz - 1):
                total += recv3[part, k].astype(F32)
            grad_ref[:, halves[part]] = total

        write_back.wait()
        for part in range(2):
            for distance, copy in kv[part]:
                @pl.when(me + distance < blocks)
                def _():
                    copy.wait_send()
            for copy in first_copies[part] + second_copies[part] + third_copies[part]:
                copy.wait_send()
        for copy in gather_x + gather_y + gather_z:
            copy.wait_send()

    return kernel


def body(query_rows, key_rows, value_rows, frame_counts, history, offsets, cotangent):
    tok, feat = query_rows.shape
    tiles = history.shape[0]
    outs = cotangent.shape[1]
    blocks = lax.axis_size("tm")
    nz = blocks // (NX * NY)
    rows = outs // blocks
    half = feat // 2
    clip_rows = tiles * blocks
    total_rows = clip_rows + tok
    lines = tiles * feat // 128
    dma = pltpu.SemaphoreType.DMA
    anywhere = pl.BlockSpec(memory_space=pl.ANY)
    vmem = pl.BlockSpec(memory_space=pltpu.VMEM)
    return pl.pallas_call(
        make_kernel(blocks, tok, feat, tiles, outs),
        out_shape=(
            jax.ShapeDtypeStruct((tok, feat), BF16),
            jax.ShapeDtypeStruct((rows, feat), F32),
        ),
        in_specs=[
            pl.BlockSpec(memory_space=pltpu.SMEM),
            anywhere,
            anywhere,
            anywhere,
            anywhere,
            vmem,
            anywhere,
        ],
        out_specs=(anywhere, vmem),
        scratch_shapes=[
            pltpu.VMEM((tok, feat), BF16),
            pltpu.VMEM((WINB, tok, feat), BF16),
            pltpu.VMEM((WINB, tok, feat), BF16),
            pltpu.VMEM((total_rows, outs), BF16),
            pltpu.VMEM((NX, NY, nz, rows, total_rows), BF16),
            pltpu.VMEM((total_rows, feat), BF16),
            pltpu.VMEM((blocks, lines, 128), BF16),
            pltpu.VMEM((blocks, lines, 128), F32),
            pltpu.VMEM((2, 3, 4, nz, rows, half), BF16),
            pltpu.VMEM((2, 3, 4, nz, rows, half), BF16),
            pltpu.VMEM((2, 4, nz, rows, half), F32),
            pltpu.VMEM((2, 3, nz, rows, half), BF16),
            pltpu.VMEM((2, 3, nz, rows, half), BF16),
            pltpu.VMEM((2, nz, rows, half), F32),
            pltpu.VMEM((2, nz - 1, rows, half), BF16),
            pltpu.VMEM((2, nz - 1, rows, half), BF16),
            pltpu.VMEM((2, nz, rows, half), F32),
            dma((6,)),
            dma((12,)),
            dma((12,)),
            dma((6 + nz - 1,)),
            dma((6 + nz - 1,)),
            dma((2, 3)),
            dma((2, 3)),
            dma((2, 3)),
            dma((2, 3)),
            dma((2, nz - 1)),
            dma((2, nz - 1)),
        ],
        compiler_params=pltpu.CompilerParams(
            collective_id=0, has_side_effects=True, vmem_limit_bytes=48 << 20
        ),
    )(
        frame_counts,
        query_rows,
        key_rows,
        value_rows,
        history.reshape(lines, 128),
        offsets,
        cotangent,
    )


def solution(mesh):
    in_specs = (
        P("tm", "head"),
        P("tm", "head"),
        P("tm", "head"),
        P(),
        P("tm", "head"),
        P("tm", None),
        P("tm", None),
    )
    out_specs = (P("tm", "head"), P("tm", "head"))
    return jax.shard_map(body, mesh=mesh, in_specs=in_specs, out_specs=out_specs, check_vma=False)
```

time: 1640 us -> 110 us (0.07)
  the two profiles are of different devices: /device:TPU:256 before, /device:TPU:272 now
where the time goes in v1:
time: 110 us
  Pallas kernels  101 us (92%)
  local copies, waits for them, and re-layouts  7.76 us (7%)
    pallas_call x1, Pallas kernels, body(): pl.pallas_call(make_kernel(blocks, tok, feat, tiles, outs), out_shape=(ja...  101 us
    unnamed x14, local copies, waits for them, and re-layouts  7.07 us

profile of v1, /device:TPU:272, one launch (start us, length us, event | category | flops | bytes accessed | tf_op | source)
XLA Modules:
  0.0 109.9 jit_solution(14297885515457170288)
XLA Ops:
  0.6 0.7 reshape.7.history
  1.3 0.0 copy-start
  1.3 1.6 %copy-done = bf16[512,2048]{1,0:T(8,128)(2,1)S(1)} copy-done((bf16[512,2048]{1,0:T(8,128)(2,1)S(1)}, bf16[512,2048]{1,0:T(8,128)(2,1)}, u32[]{:S(2)}) %copy-start) | copy-done | bytes 2097176
  2.9 0.0 copy-start.1
  2.9 0.9 copy-done.1
  3.9 0.0 copy-start.2
  3.9 0.9 copy-done.2
  4.8 0.0 copy-start.3
  4.8 0.9 copy-done.3
  5.8 0.0 copy-start.4
  5.8 0.7 copy-done.4
  6.4 0.0 copy-start.5
  6.4 0.7 copy-done.5
  7.1 101.5 %shard_map.86 = (bf16[256,512]{1,0:T(8,128)(2,1)S(1)}, f32[16,512]{1,0:T(8,128)S(1)}) custom-call(s32[128]{0:T(128)S(1)} %copy-done.4, bf16[256,512]{1,0:T(8,128)(2,1)S(1)} %copy-done.1, bf16[256,512]{1,0:T(8,128)(2,1)S(1)} %copy-done.2, bf16[256,512]{1,0:T(8,128)(2,1)S(1)} %copy-done.3, bf16[8,128]{1,0:T(8,128)(2,1)S(1)} %reshape.7.history, ...), custom_call_target="tpu_custom_call" | custom-call | tf_op jit(solution)/shard_map/pallas_call | solution.py:334
  108.5 0.7 copy.11
  109.2 0.6 copy.12
Async XLA Ops:
  1.3 1.6 %copy-start = (bf16[512,2048]{1,0:T(8,128)(2,1)S(1)}, bf16[512,2048]{1,0:T(8,128)(2,1)}, u32[]{:S(2)}) copy-start(bf16[512,2048]{1,0:T(8,128)(2,1)} %cot_hbm.1) | copy-start | bytes 6291460
  2.9 0.9 copy-start.1
  3.9 0.9 copy-start.2
  4.8 0.9 copy-start.3
  5.8 0.7 copy-start.4
  6.4 0.7 copy-start.5

commit v2 on v1

v2 whole, which is shorter than its diff:
```python
import math

import jax
import jax.numpy as jnp
from jax import lax
from jax.experimental import pallas as pl
from jax.experimental.pallas import tpu as pltpu
from jax.sharding import PartitionSpec as P

HD = 128
TPF = 64
WINB = 4
NX = 4
NY = 4
STREAMS = (0, 1)
MESH = pl.DeviceIdType.MESH
F32 = jnp.float32
BF16 = jnp.bfloat16


def remote(src, dst, send, recv, target):
    return pltpu.make_async_remote_copy(
        src_ref=src,
        dst_ref=dst,
        send_sem=send,
        recv_sem=recv,
        device_id={"tm": target},
        device_id_type=MESH,
    )


def make_kernel(blocks, tok, feat, tiles, outs, streams):
    nz = blocks // (NX * NY)
    half = feat // 2
    halves = (slice(0, half), slice(half, feat))
    heads = feat // HD
    rows = outs // blocks
    plane = outs // NX
    scale = 1.0 / math.sqrt(HD)

    def kernel(
        counts, query_hbm, key_hbm, value_hbm, history, offsets, cot_hbm,
        attended_ref, grad_ref,
        query, keys, values, mixed, cot, cot_t, clip, hist_all, hist_f32,
        local_sem, row_send, row_recv, kv_send, kv_recv, out_send, out_recv, ag_send, ag_recv,
        *stream_refs,
    ):
        me = lax.axis_index("tm")
        refs = [stream_refs[13 * i : 13 * (i + 1)] for i in range(len(streams))]
        x = lax.rem(me, NX)
        y = lax.rem(me // NX, NY)
        z = me // (NX * NY)

        def at_x(k):
            return me - x + lax.rem(x + k, NX)

        def at_y(k):
            return me + (lax.rem(y + k, NY) - y) * NX

        def at_z(k):
            return me + (lax.rem(z + k, nz) - z) * (NX * NY)

        has_before = me >= NX
        has_after = me + NX < blocks
        peers = [at_x(k) for k in range(1, NX)]
        peers += [at_y(k) for k in range(1, NY)]
        peers += [at_z(k) for k in range(1, nz)]

        def columns(head):
            return pl.ds(pl.multiple_of(head * HD, HD), HD)

        own_head = columns(x)
        last = WINB - 1
        local = [
            pltpu.make_async_copy(cot_hbm, cot, local_sem.at[0]),
            pltpu.make_async_copy(query_hbm.at[:, own_head], query.at[x], local_sem.at[1]),
            pltpu.make_async_copy(key_hbm.at[:, own_head], keys.at[last + x], local_sem.at[2]),
            pltpu.make_async_copy(value_hbm.at[:, own_head], values.at[last + x], local_sem.at[3]),
            pltpu.make_async_copy(
                history, hist_all.at[(y * NX + x) * nz + z], local_sem.at[4]
            ),
        ]
        for copy in local:
            copy.start()

        barrier = pltpu.get_barrier_semaphore()
        for peer in peers:
            pl.semaphore_signal(barrier, inc=1, device_id={"tm": peer}, device_id_type=MESH)
        @pl.when(has_before)
        def _():
            pl.semaphore_signal(
                barrier, inc=1, device_id={"tm": me - NX}, device_id_type=MESH
            )

        @pl.when(has_after)
        def _():
            pl.semaphore_signal(
                barrier, inc=1, device_id={"tm": me + NX}, device_id_type=MESH
            )

        around = has_before.astype(jnp.int32) + has_after.astype(jnp.int32)
        pl.semaphore_wait(barrier, len(peers) + around)

        swaps = []
        for which, (src, dst, first) in enumerate(
            ((key_hbm, keys, last), (value_hbm, values, last), (query_hbm, query, 0))
        ):
            swaps.append(
                [
                    remote(
                        src.at[:, columns(lax.rem(x + k, NX))],
                        dst.at[first + x],
                        kv_send.at[which * (NX - 1) + k - 1],
                        kv_recv.at[which * (NX - 1) + k - 1],
                        at_x(k),
                    )
                    for k in range(1, NX)
                ]
            )
        forward = [
            remote(
                ref.at[WINB : WINB + NX - 1],
                ref.at[0 : NX - 1],
                row_send.at[which],
                row_recv.at[which],
                lax.rem(me + NX, blocks),
            )
            for which, ref in enumerate((keys, values))
        ]

        def gather(first, width, slot, targets):
            block = hist_all.at[pl.ds(first, width)]
            copies = []
            for i, target in enumerate(targets):
                copies.append(
                    remote(block, block, ag_send.at[slot + i], ag_recv.at[slot + i], target)
                )
            return copies

        column = (y * NX + x) * nz
        gather_z = gather(column + z, 1, 6, [at_z(k) for k in range(1, nz)])
        gather_x = gather(column, nz, 0, [at_x(k) for k in range(1, NX)])
        gather_y = gather(y * NX * nz, NX * nz, 3, [at_y(k) for k in range(1, NY)])

        def start(copies):
            for copy in copies:
                copy.start()

        def arrive(copies):
            for copy in copies:
                copy.wait_recv()

        local[4].wait()
        start(gather_z)
        start(swaps[0])
        start(swaps[1])

        @pl.when(jnp.logical_not(has_before))
        def _():
            keys[0 : NX - 1] = jnp.zeros((NX - 1, tok, HD), BF16)
            values[0 : NX - 1] = jnp.zeros((NX - 1, tok, HD), BF16)

        def turn(c, _):
            block = cot[:, pl.ds(pl.multiple_of(c * 128, 128), 128)].T
            for e in range(128 // (NX * rows)):
                zy = c * (128 // (NX * rows)) + e
                to_y = lax.rem(lax.rem(zy, NY) + NY - y, NY)
                to_z = lax.rem(zy // NY + nz - z, nz)
                for i in range(NX):
                    first = (e * NX + i) * rows
                    cot_t[lax.rem(i + NX - x, NX), to_y, to_z] = block[first : first + rows]
            return 0

        local[0].wait()
        turns = outs // 128
        lax.fori_loop(0, turns // 2, turn, 0)
        local[2].wait()
        arrive(swaps[0])
        pl.when(has_after)(forward[0].start)
        start(swaps[2])
        arrive(gather_z)
        start(gather_x)
        local[3].wait()
        arrive(swaps[1])
        pl.when(has_after)(forward[1].start)
        lax.fori_loop(turns // 2, turns, turn, 0)

        kept = []
        frame = lax.broadcasted_iota(jnp.int32, (1, tok), 1) // TPF
        for slot in range(last + NX):
            source = me - x - last + slot
            count = jnp.where(source >= 0, counts[jnp.maximum(source, 0)], 0)
            kept.append(frame < count)

        clip_rows = tiles * blocks
        tile = jnp.bitwise_and(me - offsets[...], blocks - 1)
        tile = lax.rem(tile, NX * NY) * nz + tile // (NX * NY)
        spread = (
            lax.broadcasted_iota(jnp.int32, (blocks, clip_rows), 1) // tiles
            == lax.broadcasted_iota(jnp.int32, (blocks, clip_rows), 0)
        )
        spread = jnp.where(spread, 1.0, 0.0).astype(BF16)
        source_tile = jnp.dot(
            jnp.broadcast_to(tile.astype(F32).astype(BF16), (16, blocks)),
            spread,
            preferred_element_type=F32,
        )[0:1]
        hist_row = lax.broadcasted_iota(jnp.int32, (clip_rows, clip_rows), 0)
        clip_row = lax.broadcasted_iota(jnp.int32, (clip_rows, clip_rows), 1)
        chosen = (lax.rem(hist_row, blocks).astype(F32) == source_tile) & (
            hist_row // blocks == lax.rem(clip_row, tiles)
        )
        chosen = jnp.where(chosen, 1.0, 0.0).astype(BF16)

        arrive(gather_x)
        start(gather_y)

        def attend(i):
            key_head = keys[i : i + WINB].reshape(WINB * tok, HD)
            value_head = values[i : i + WINB].reshape(WINB * tok, HD)
            scores = lax.dot_general(
                query[i], key_head, (((1,), (1,)), ((), ())), preferred_element_type=F32
            )
            seen = jnp.concatenate(kept[i : i + WINB], axis=1)
            scores = jnp.where(seen, scores * scale, -jnp.inf)
            weights = jnp.exp(scores - jnp.max(scores, axis=1, keepdims=True))
            probs = weights * (1.0 / jnp.sum(weights, axis=1, keepdims=True))
            mixed[i] = jnp.dot(
                probs.astype(BF16), value_head, preferred_element_type=F32
            ).astype(BF16)

        attended = clip.at[clip_rows : clip_rows + tok]
        backs = [
            remote(
                mixed.at[i],
                attended.at[:, own_head],
                out_send.at[i],
                out_recv.at[x],
                me - x + i,
            )
            for i in range(NX)
        ]
        stay = pltpu.make_async_copy(mixed.at[x], attended.at[:, own_head], local_sem.at[1])
        local[1].wait()
        arrive(swaps[2])
        for i in range(NX - 1, -1, -1):
            if i == NX - 2:
                pl.when(has_before)(forward[0].wait_recv)
                pl.when(has_before)(forward[1].wait_recv)
            attend(i)
            pl.when(x != i)(backs[i].start)
        stay.start()

        arrive(gather_y)
        hist_f32[...] = hist_all[...].astype(F32)
        pieces = []
        for t in range(tiles):
            line = [hist_f32[:, t * heads + c, :] for c in range(heads)]
            pieces.append(jnp.concatenate(line, axis=1))
        hist_rows = jnp.concatenate(pieces, axis=0).astype(BF16)
        clip[0:clip_rows] = lax.dot_general(
            chosen, hist_rows, (((0,), (0,)), ((), ())), preferred_element_type=F32
        ).astype(BF16)
        for k in range(1, NX):
            other = lax.rem(x + k, NX)
            remote(
                mixed.at[0], attended.at[:, columns(other)], out_send.at[0], out_recv.at[other], at_x(k)
            ).wait_recv()
        stay.wait()

        reach = (at_x, at_y)
        sends = []

        def send(src, dst, send_sem, recv_sem, target):
            copy = remote(src, dst, send_sem, recv_sem, target)
            copy.start()
            sends.append(copy)
            return copy

        stage1 = [[[None] * 4 for _ in range(3)] for _ in streams]
        stage2 = [[None] * 3 for _ in streams]
        stage3 = [[None] * (nz - 1) for _ in streams]

        def product(i, k):
            s1, r1, own1, s1_sem, r1_sem = refs[i][0], refs[i][1], refs[i][2], refs[i][7], refs[i][8]
            left = cot_t[k] if streams[i] == 0 else cot_t[:, k]
            block = jnp.dot(
                left.reshape(outs // 4, clip_rows + tok),
                clip[:, halves[i]],
                preferred_element_type=F32,
            ).reshape(4, nz, rows, half)
            if k == 0:
                own1[...] = block
                return
            s1[k - 1] = block.astype(BF16)
            for j in (1, 2, 3, 0):
                stage1[i][k - 1][j] = send(
                    s1.at[k - 1, j],
                    r1.at[k - 1, j],
                    s1_sem.at[k - 1, j],
                    r1_sem.at[k - 1, j],
                    reach[streams[i]](k),
                )

        def second(i, j):
            r1, own1, s2, r2 = refs[i][1], refs[i][2], refs[i][3], refs[i][4]
            for k in range(3):
                stage1[i][k][j].wait_recv()
            total = own1[j]
            for k in range(3):
                total += r1[k, j].astype(F32)
            if j == 0:
                own1[0] = total
                return
            s2[j - 1] = total.astype(BF16)
            stage2[i][j - 1] = send(
                s2.at[j - 1],
                r2.at[j - 1],
                refs[i][9].at[j - 1],
                refs[i][10].at[j - 1],
                reach[1 - streams[i]](j),
            )

        def third(i):
            own1, r2, s3, r3 = refs[i][2], refs[i][4], refs[i][5], refs[i][6]
            arrive(stage2[i])
            total = own1[0]
            for k in range(3):
                total += r2[k].astype(F32)
            own1[1, 0] = total[0]
            s3[...] = total[1:].astype(BF16)
            for k in range(1, nz):
                stage3[i][k - 1] = send(
                    s3.at[k - 1],
                    r3.at[k - 1],
                    refs[i][11].at[k - 1],
                    refs[i][12].at[k - 1],
                    at_z(k),
                )

        def finish(i):
            arrive(stage3[i])
            total = refs[i][2][1, 0]
            for k in range(nz - 1):
                total += refs[i][6][k].astype(F32)
            grad_ref[:, halves[i]] = total

        every = range(len(streams))
        for k in (1, 2, 3, 0):
            for i in every:
                product(i, k)
        write_back = pltpu.make_async_copy(
            attended, attended_ref, local_sem.at[5]
        )
        write_back.start()
        for j in (1, 2, 3, 0):
            for i in every:
                second(i, j)
        for i in every:
            third(i)
        for i in every:
            finish(i)

        write_back.wait()
        for copy in forward:
            pl.when(has_after)(copy.wait_send)
        for i in range(NX):
            pl.when(x != i)(backs[i].wait_send)
        for copy in swaps[0] + swaps[1] + swaps[2] + gather_x + gather_y + gather_z + sends:
            copy.wait_send()

    return kernel


def body(query_rows, key_rows, value_rows, frame_counts, history, offsets, cotangent):
    tok, feat = query_rows.shape
    tiles = history.shape[0]
    outs = cotangent.shape[1]
    blocks = lax.axis_size("tm")
    nz = blocks // (NX * NY)
    rows = outs // blocks
    half = feat // 2
    clip_rows = tiles * blocks
    total_rows = clip_rows + tok
    lines = tiles * feat // 128
    dma = pltpu.SemaphoreType.DMA
    anywhere = pl.BlockSpec(memory_space=pltpu.HBM)
    vmem = pl.BlockSpec(memory_space=pltpu.VMEM)
    streams = STREAMS
    width = half
    stream_scratch = []
    for _ in streams:
        stream_scratch += [
            pltpu.VMEM((3, 4, nz, rows, width), BF16),
            pltpu.VMEM((3, 4, nz, rows, width), BF16),
            pltpu.VMEM((4, nz, rows, width), F32),
            pltpu.VMEM((3, nz, rows, width), BF16),
            pltpu.VMEM((3, nz, rows, width), BF16),
            pltpu.VMEM((nz - 1, rows, width), BF16),
            pltpu.VMEM((nz - 1, rows, width), BF16),
            dma((3, 4)),
            dma((3, 4)),
            dma((3,)),
            dma((3,)),
            dma((nz - 1,)),
            dma((nz - 1,)),
        ]
    return pl.pallas_call(
        make_kernel(blocks, tok, feat, tiles, outs, streams),
        out_shape=(
            jax.ShapeDtypeStruct((tok, feat), BF16),
            jax.ShapeDtypeStruct((rows, feat), F32),
        ),
        in_specs=[
            pl.BlockSpec(memory_space=pltpu.SMEM),
            anywhere,
            anywhere,
            anywhere,
            anywhere,
            vmem,
            anywhere,
        ],
        out_specs=(anywhere, vmem),
        scratch_shapes=[
            pltpu.VMEM((NX, tok, HD), BF16),
            pltpu.VMEM((WINB - 1 + NX, tok, HD), BF16),
            pltpu.VMEM((WINB - 1 + NX, tok, HD), BF16),
            pltpu.VMEM((NX, tok, HD), BF16),
            pltpu.VMEM((total_rows, outs), BF16),
            pltpu.VMEM((NX, NY, nz, rows, total_rows), BF16),
            pltpu.VMEM((total_rows, feat), BF16),
            pltpu.VMEM((blocks, lines, 128), BF16),
            pltpu.VMEM((blocks, lines, 128), F32),
            dma((6,)),
            dma((2,)),
            dma((2,)),
            dma((9,)),
            dma((9,)),
            dma((NX,)),
            dma((NX,)),
            dma((6 + nz - 1,)),
            dma((6 + nz - 1,)),
        ]
        + stream_scratch,
        compiler_params=pltpu.CompilerParams(
            collective_id=0, has_side_effects=True, vmem_limit_bytes=60 << 20
        ),
    )(
        frame_counts,
        query_rows,
        key_rows,
        value_rows,
        history.reshape(lines, 128),
        offsets,
        cotangent,
    )


def solution(mesh):
    in_specs = (
        P("tm", "head"),
        P("tm", "head"),
        P("tm", "head"),
        P(),
        P("tm", "head"),
        P("tm", None),
        P("tm", None),
    )
    out_specs = (P("tm", "head"), P("tm", "head"))
    return jax.shard_map(body, mesh=mesh, in_specs=in_specs, out_specs=out_specs, check_vma=False)
```

time: 110 us -> 66 us (0.60)
  the two profiles are of different devices: /device:TPU:272 before, /device:TPU:256 now
where the time goes in v2:
time: 66 us; the launch traced here: 65.7 us
  Pallas kernels  60.8 us (92%)
  local copies, waits for them, and re-layouts  4.31 us (7%)
    pallas_call x1, Pallas kernels, body(): pl.pallas_call(make_kernel(blocks, tok, feat, tiles, outs, streams), out_...  60.8 us
    unnamed x2, local copies, waits for them, and re-layouts  3.04 us

profile of v2, /device:TPU:256, one launch (start us, length us, event | category | flops | bytes accessed | tf_op | source)
XLA Modules:
  0.0 65.7 jit_solution(11185406208752321563)
XLA Ops:
  0.6 1.3 %reshape.7.history = bf16[8,128]{1,0:T(8,128)(2,1)} reshape(bf16[2,512]{1,0:T(2,128)(2,1)} %param.11) | data formatting | bytes 4096 | tf_op jit(solution)/shard_map/reshape | solution.py:453
  1.9 60.8 %shard_map.86 = (bf16[256,512]{1,0:T(8,128)(2,1)}, f32[16,512]{1,0:T(8,128)}) custom-call(s32[128]{0:T(128)} %counts.1, bf16[256,512]{1,0:T(8,128)(2,1)} %query_hbm.1, bf16[256,512]{1,0:T(8,128)(2,1)} %key_hbm.1, bf16[256,512]{1,0:T(8,128)(2,1)} %value_hbm.1, bf16[8,128]{1,0:T(8,128)(2,1)} %reshape.7.history, s32[1,128]{1,0:T(1,128)} %offsets.1, ...), custom_call_target="tpu_custom_call" | custom-call | tf_op jit(solution)/shard_map/pallas_call | solution.py:408
  62.7 1.7 %copy.11 = bf16[256,512]{1,0:T(8,128)(2,1)} copy(bf16[256,512]{1,0:T(8,128)(2,1)} %get-tuple-element.4) | data formatting | bytes 524288
  64.3 1.4 %copy.12 = f32[16,512]{1,0:T(8,128)} copy(f32[16,512]{1,0:T(8,128)} %get-tuple-element.5) | data formatting | bytes 65536

commit v3 on v2

--- a/solution.py
+++ b/solution.py
@@ -42,11 +42,11 @@
         counts, query_hbm, key_hbm, value_hbm, history, offsets, cot_hbm,
         attended_ref, grad_ref,
         query, keys, values, mixed, cot, cot_t, clip, hist_all, hist_f32,
-        local_sem, row_send, row_recv, kv_send, kv_recv, out_send, out_recv, ag_send, ag_recv,
+        local_sem, row_send, row_recv, ahead_send, ahead_recv, kv_send, kv_recv, out_send, out_recv, ag_send, ag_recv,
         *stream_refs,
     ):
         me = lax.axis_index("tm")
-        refs = [stream_refs[13 * i : 13 * (i + 1)] for i in range(len(streams))]
+        refs = [stream_refs[18 * i : 18 * (i + 1)] for i in range(len(streams))]
         x = lax.rem(me, NX)
         y = lax.rem(me // NX, NY)
         z = me // (NX * NY)
@@ -76,9 +76,6 @@
             pltpu.make_async_copy(query_hbm.at[:, own_head], query.at[x], local_sem.at[1]),
             pltpu.make_async_copy(key_hbm.at[:, own_head], keys.at[last + x], local_sem.at[2]),
             pltpu.make_async_copy(value_hbm.at[:, own_head], values.at[last + x], local_sem.at[3]),
-            pltpu.make_async_copy(
-                history, hist_all.at[(y * NX + x) * nz + z], local_sem.at[4]
-            ),
         ]
         for copy in local:
             copy.start()
@@ -88,18 +85,12 @@
             pl.semaphore_signal(barrier, inc=1, device_id={"tm": peer}, device_id_type=MESH)
         @pl.when(has_before)
         def _():
-            pl.semaphore_signal(
-                barrier, inc=1, device_id={"tm": me - NX}, device_id_type=MESH
-            )
-
-        @pl.when(has_after)
-        def _():
-            pl.semaphore_signal(
-                barrier, inc=1, device_id={"tm": me + NX}, device_id_type=MESH
-            )
-
-        around = has_before.astype(jnp.int32) + has_after.astype(jnp.int32)
-        pl.semaphore_wait(barrier, len(peers) + around)
+            for i in range(NX):
+                pl.semaphore_signal(
+                    barrier, inc=1, device_id={"tm": me - x - NX + i}, device_id_type=MESH
+                )
+
+        pl.semaphore_wait(barrier, len(peers) + jnp.where(has_after, NX, 0))
 
         swaps = []
         for which, (src, dst, first) in enumerate(
@@ -117,16 +108,34 @@
                     for k in range(1, NX)
                 ]
             )
-        forward = [
+        ahead = [
             remote(
-                ref.at[WINB : WINB + NX - 1],
-                ref.at[0 : NX - 1],
-                row_send.at[which],
-                row_recv.at[which],
-                lax.rem(me + NX, blocks),
+                key_hbm.at[:, i * HD : (i + 1) * HD],
+                keys.at[jnp.maximum(x - 1, 0)],
+                ahead_send.at[i],
+                ahead_recv.at[jnp.maximum(x - 1, 0)],
+                lax.rem(me - x + NX + i, blocks),
             )
-            for which, ref in enumerate((keys, values))
+            for i in range(NX)
         ]
+        sends_ahead = has_after & (x > 0)
+        forward = remote(
+            values.at[WINB : WINB + NX - 1],
+            values.at[0 : NX - 1],
+            row_send.at[0],
+            row_recv.at[0],
+            lax.rem(me + NX, blocks),
+        )
+
+        def arrive_ahead():
+            for i in range(NX - 1):
+                remote(
+                    key_hbm.at[:, 0:HD],
+                    keys.at[i],
+                    ahead_send.at[i],
+                    ahead_recv.at[i],
+                    lax.rem(me + NX, blocks),
+                ).wait_recv()
 
         def gather(first, width, slot, targets):
             block = hist_all.at[pl.ds(first, width)]
@@ -150,10 +159,21 @@
             for copy in copies:
                 copy.wait_recv()
 
-        local[4].wait()
+        line = history[...].astype(F32)
+        hist_all[column + z] = jnp.concatenate(
+            [line[t : t + 1, c * 128 : (c + 1) * 128] for t in range(tiles) for c in range(heads)],
+            axis=0,
+        ).astype(BF16)
         start(gather_z)
+        start(swaps[1])
+
+        @pl.when(sends_ahead)
+        def _():
+            for copy in ahead:
+                copy.start()
+
         start(swaps[0])
-        start(swaps[1])
+        start(swaps[2])
 
         @pl.when(jnp.logical_not(has_before))
         def _():
@@ -174,15 +194,11 @@
         local[0].wait()
         turns = outs // 128
         lax.fori_loop(0, turns // 2, turn, 0)
-        local[2].wait()
-        arrive(swaps[0])
-        pl.when(has_after)(forward[0].start)
-        start(swaps[2])
+        local[3].wait()
+        arrive(swaps[1])
+        pl.when(has_after)(forward.start)
         arrive(gather_z)
         start(gather_x)
-        local[3].wait()
-        arrive(swaps[1])
-        pl.when(has_after)(forward[1].start)
         lax.fori_loop(turns // 2, turns, turn, 0)
 
         kept = []
@@ -242,11 +258,13 @@
         ]
         stay = pltpu.make_async_copy(mixed.at[x], attended.at[:, own_head], local_sem.at[1])
         local[1].wait()
+        local[2].wait()
+        arrive(swaps[0])
         arrive(swaps[2])
         for i in range(NX - 1, -1, -1):
             if i == NX - 2:
-                pl.when(has_before)(forward[0].wait_recv)
-                pl.when(has_before)(forward[1].wait_recv)
+                pl.when(has_before)(arrive_ahead)
+                pl.when(has_before)(forward.wait_recv)
             attend(i)
             pl.when(x != i)(backs[i].start)
         stay.start()
@@ -277,38 +295,66 @@
             sends.append(copy)
             return copy
 
-        stage1 = [[[None] * 4 for _ in range(3)] for _ in streams]
         stage2 = [[None] * 3 for _ in streams]
         stage3 = [[None] * (nz - 1) for _ in streams]
-
-        def product(i, k):
-            s1, r1, own1, s1_sem, r1_sem = refs[i][0], refs[i][1], refs[i][2], refs[i][7], refs[i][8]
+        relays = [[None] * 4 for _ in streams]
+        direct = [[[None] * 4 for _ in range(2)] for _ in streams]
+
+        def dot1(i, k):
             left = cot_t[k] if streams[i] == 0 else cot_t[:, k]
-            block = jnp.dot(
+            return jnp.dot(
                 left.reshape(outs // 4, clip_rows + tok),
                 clip[:, halves[i]],
                 preferred_element_type=F32,
             ).reshape(4, nz, rows, half)
-            if k == 0:
-                own1[...] = block
-                return
-            s1[k - 1] = block.astype(BF16)
+
+        up, down = (1, 3), (2, 0)
+
+        def opposite(i):
+            s0, r0 = refs[i][13], refs[i][14]
+            s0[...] = dot1(i, 2).astype(BF16)
             for j in (1, 2, 3, 0):
-                stage1[i][k - 1][j] = send(
-                    s1.at[k - 1, j],
-                    r1.at[k - 1, j],
-                    s1_sem.at[k - 1, j],
-                    r1_sem.at[k - 1, j],
-                    reach[streams[i]](k),
+                relays[i][j] = send(
+                    s0.at[j],
+                    r0.at[j],
+                    refs[i][15].at[j],
+                    refs[i][16].at[j],
+                    reach[streams[i]](1 if j in up else 3),
                 )
+
+        def pass1(i, side, js):
+            s1, r1, s1_sem, r1_sem = refs[i][0], refs[i][1], refs[i][7], refs[i][8]
+            for j in js:
+                direct[i][side][j] = send(
+                    s1.at[side, j],
+                    r1.at[side, j],
+                    s1_sem.at[side, j],
+                    r1_sem.at[side, j],
+                    reach[streams[i]](1 if side == 0 else 3),
+                )
+
+        def beside(i, side):
+            block = dot1(i, 1 if side == 0 else 3)
+            through = up if side == 0 else down
+            for j in range(4):
+                if j in through:
+                    refs[i][17][j] = block[j]
+                else:
+                    refs[i][0][side, j] = block[j].astype(BF16)
+            pass1(i, side, down if side == 0 else up)
+
+        def through1(i, side):
+            for j in up if side == 0 else down:
+                relays[i][j].wait_recv()
+                total = refs[i][17][j] + refs[i][14][j].astype(F32)
+                refs[i][0][side, j] = total.astype(BF16)
+                pass1(i, side, (j,))
 
         def second(i, j):
             r1, own1, s2, r2 = refs[i][1], refs[i][2], refs[i][3], refs[i][4]
-            for k in range(3):
-                stage1[i][k][j].wait_recv()
-            total = own1[j]
-            for k in range(3):
-                total += r1[k, j].astype(F32)
+            direct[i][0][j].wait_recv()
+            direct[i][1][j].wait_recv()
+            total = own1[j] + r1[0, j].astype(F32) + r1[1, j].astype(F32)
             if j == 0:
                 own1[0] = total
                 return
@@ -346,9 +392,16 @@
             grad_ref[:, halves[i]] = total
 
         every = range(len(streams))
-        for k in (1, 2, 3, 0):
+        for i in every:
+            opposite(i)
+        for side in range(2):
             for i in every:
-                product(i, k)
+                beside(i, side)
+        for i in every:
+            refs[i][2][...] = dot1(i, 0)
+        for side in range(2):
+            for i in every:
+                through1(i, side)
         write_back = pltpu.make_async_copy(
             attended, attended_ref, local_sem.at[5]
         )
@@ -362,14 +415,20 @@
             finish(i)
 
         write_back.wait()
-        for copy in forward:
-            pl.when(has_after)(copy.wait_send)
+        pl.when(has_after)(forward.wait_send)
+        for copy in ahead:
+            pl.when(sends_ahead)(copy.wait_send)
         for i in range(NX):
             pl.when(x != i)(backs[i].wait_send)
         for copy in swaps[0] + swaps[1] + swaps[2] + gather_x + gather_y + gather_z + sends:
             copy.wait_send()
 
     return kernel
+
+
+def hand_on(attended, grad, attended_out, grad_out):
+    attended_out[...] = attended[...]
+    grad_out[...] = grad[...]
 
 
 def body(query_rows, key_rows, value_rows, frame_counts, history, offsets, cotangent):
@@ -391,21 +450,26 @@
     stream_scratch = []
     for _ in streams:
         stream_scratch += [
-            pltpu.VMEM((3, 4, nz, rows, width), BF16),
-            pltpu.VMEM((3, 4, nz, rows, width), BF16),
+            pltpu.VMEM((2, 4, nz, rows, width), BF16),
+            pltpu.VMEM((2, 4, nz, rows, width), BF16),
             pltpu.VMEM((4, nz, rows, width), F32),
             pltpu.VMEM((3, nz, rows, width), BF16),
             pltpu.VMEM((3, nz, rows, width), BF16),
             pltpu.VMEM((nz - 1, rows, width), BF16),
             pltpu.VMEM((nz - 1, rows, width), BF16),
-            dma((3, 4)),
-            dma((3, 4)),
+            dma((2, 4)),
+            dma((2, 4)),
             dma((3,)),
             dma((3,)),
             dma((nz - 1,)),
             dma((nz - 1,)),
+            pltpu.VMEM((4, nz, rows, width), BF16),
+            pltpu.VMEM((4, nz, rows, width), BF16),
+            dma((4,)),
+            dma((4,)),
+            pltpu.VMEM((4, nz, rows, width), F32),
         ]
-    return pl.pallas_call(
+    results = pl.pallas_call(
         make_kernel(blocks, tok, feat, tiles, outs, streams),
         out_shape=(
             jax.ShapeDtypeStruct((tok, feat), BF16),
@@ -416,7 +480,7 @@
             anywhere,
             anywhere,
             anywhere,
-            anywhere,
+            vmem,
             vmem,
             anywhere,
         ],
@@ -432,8 +496,10 @@
             pltpu.VMEM((blocks, lines, 128), BF16),
             pltpu.VMEM((blocks, lines, 128), F32),
             dma((6,)),
-            dma((2,)),
-            dma((2,)),
+            dma((1,)),
+            dma((1,)),
+            dma((NX,)),
+            dma((NX - 1,)),
             dma((9,)),
             dma((9,)),
             dma((NX,)),
@@ -450,10 +516,19 @@
         query_rows,
         key_rows,
         value_rows,
-        history.reshape(lines, 128),
+        history,
         offsets,
         cotangent,
     )
+    return pl.pallas_call(
+        hand_on,
+        out_shape=(
+            jax.ShapeDtypeStruct((tok, feat), BF16),
+            jax.ShapeDtypeStruct((rows, feat), F32),
+        ),
+        in_specs=[vmem, vmem],
+        out_specs=(vmem, vmem),
+    )(*results)
 
 
 def solution(mesh):

time: 66 us -> 61 us (0.924)
  local copies, waits for them, and re-layouts: 4.31 us -> 0 us
    unnamed x2 -> x0, local copies, waits for them, and re-layouts: 3.04 us -> none
    pallas_call x1, Pallas kernels: 60.8 us -> 58.5 us  [body(): pl.pallas_call(make_kernel(blocks, tok, feat, tiles, outs, streams), out_...]
    pallas_call x0 -> x1, Pallas kernels: none -> 1.68 us  [body(): pl.pallas_call(hand_on, out_shape=(jax.ShapeDtypeStruct((tok, feat), BF16...]
    reshape x1 -> x0, local copies, waits for them, and re-layouts: 1.27 us -> none  [body(): history.reshape(lines, 128)]
where the time goes in v3:
time: 61 us; the launch traced here: 60.8 us
  Pallas kernels  60.2 us (99%)
  between operations  0.64 us (1%)
    pallas_call x1, Pallas kernels, body(): pl.pallas_call(make_kernel(blocks, tok, feat, tiles, outs, streams), out_...  58.5 us
    pallas_call x1, Pallas kernels, body(): pl.pallas_call(hand_on, out_shape=(jax.ShapeDtypeStruct((tok, feat), BF16...  1.68 us

profile of v3, /device:TPU:256, one launch (start us, length us, event | category | flops | bytes accessed | tf_op | source)
XLA Modules:
  0.0 60.8 jit_solution(9659193711915849944)
XLA Ops:
  0.6 58.5 %shard_map.86 = (bf16[256,512]{1,0:T(8,128)(2,1)}, f32[16,512]{1,0:T(8,128)}) custom-call(s32[128]{0:T(128)} %counts.1, bf16[256,512]{1,0:T(8,128)(2,1)} %query_hbm.1, bf16[256,512]{1,0:T(8,128)(2,1)} %key_hbm.1, bf16[256,512]{1,0:T(8,128)(2,1)} %value_hbm.1, bf16[2,512]{1,0:T(2,128)(2,1)} %history.1, s32[1,128]{1,0:T(1,128)} %offsets.1, ...), custom_call_target="tpu_custom_call" | custom-call | tf_op jit(solution)/shard_map/pallas_call | solution.py:472
  59.1 1.7 %shard_map.87 = (bf16[256,512]{1,0:T(8,128)(2,1)}, f32[16,512]{1,0:T(8,128)}) custom-call(bf16[256,512]{1,0:T(8,128)(2,1)} %get-tuple-element.4.attended, f32[16,512]{1,0:T(8,128)} %get-tuple-element.5.grad), custom_call_target="tpu_custom_call" | custom-call | tf_op jit(solution)/shard_map/pallas_call | solution.py:523

commit v4 on v3

--- a/solution.py
+++ b/solution.py
@@ -39,9 +39,9 @@
     scale = 1.0 / math.sqrt(HD)
 
     def kernel(
-        counts, query_hbm, key_hbm, value_hbm, history, offsets, cot_hbm,
+        counts_hbm, query_hbm, key_hbm, value_hbm, history_hbm, offsets_hbm, cot_hbm,
         attended_ref, grad_ref,
-        query, keys, values, mixed, cot, cot_t, clip, hist_all, hist_f32,
+        history, offsets, counts, query, keys, values, mixed, cot, cot_t, clip, hist_all, hist_f32,
         local_sem, row_send, row_recv, ahead_send, ahead_recv, kv_send, kv_recv, out_send, out_recv, ag_send, ag_recv,
         *stream_refs,
     ):
@@ -76,9 +76,10 @@
             pltpu.make_async_copy(query_hbm.at[:, own_head], query.at[x], local_sem.at[1]),
             pltpu.make_async_copy(key_hbm.at[:, own_head], keys.at[last + x], local_sem.at[2]),
             pltpu.make_async_copy(value_hbm.at[:, own_head], values.at[last + x], local_sem.at[3]),
+            pltpu.make_async_copy(history_hbm, history, local_sem.at[4]),
+            pltpu.make_async_copy(offsets_hbm, offsets, local_sem.at[6]),
+            pltpu.make_async_copy(counts_hbm, counts, local_sem.at[7]),
         ]
-        for copy in local:
-            copy.start()
 
         barrier = pltpu.get_barrier_semaphore()
         for peer in peers:
@@ -90,6 +91,8 @@
                     barrier, inc=1, device_id={"tm": me - x - NX + i}, device_id_type=MESH
                 )
 
+        for copy in local:
+            copy.start()
         pl.semaphore_wait(barrier, len(peers) + jnp.where(has_after, NX, 0))
 
         swaps = []
@@ -159,6 +162,7 @@
             for copy in copies:
                 copy.wait_recv()
 
+        local[4].wait()
         line = history[...].astype(F32)
         hist_all[column + z] = jnp.concatenate(
             [line[t : t + 1, c * 128 : (c + 1) * 128] for t in range(tiles) for c in range(heads)],
@@ -201,6 +205,7 @@
         start(gather_x)
         lax.fori_loop(turns // 2, turns, turn, 0)
 
+        local[6].wait()
         kept = []
         frame = lax.broadcasted_iota(jnp.int32, (1, tok), 1) // TPF
         for slot in range(last + NX):
@@ -209,6 +214,7 @@
             kept.append(frame < count)
 
         clip_rows = tiles * blocks
+        local[5].wait()
         tile = jnp.bitwise_and(me - offsets[...], blocks - 1)
         tile = lax.rem(tile, NX * NY) * nz + tile // (NX * NY)
         spread = (
@@ -411,9 +417,6 @@
                 second(i, j)
         for i in every:
             third(i)
-        for i in every:
-            finish(i)
-
         write_back.wait()
         pl.when(has_after)(forward.wait_send)
         for copy in ahead:
@@ -422,13 +425,10 @@
             pl.when(x != i)(backs[i].wait_send)
         for copy in swaps[0] + swaps[1] + swaps[2] + gather_x + gather_y + gather_z + sends:
             copy.wait_send()
+        for i in every:
+            finish(i)
 
     return kernel
-
-
-def hand_on(attended, grad, attended_out, grad_out):
-    attended_out[...] = attended[...]
-    grad_out[...] = grad[...]
 
 
 def body(query_rows, key_rows, value_rows, frame_counts, history, offsets, cotangent):
@@ -469,23 +469,15 @@
             dma((4,)),
             pltpu.VMEM((4, nz, rows, width), F32),
         ]
-    results = pl.pallas_call(
+    return pl.pallas_call(
         make_kernel(blocks, tok, feat, tiles, outs, streams),
-        out_shape=(
-            jax.ShapeDtypeStruct((tok, feat), BF16),
-            jax.ShapeDtypeStruct((rows, feat), F32),
-        ),
-        in_specs=[
-            pl.BlockSpec(memory_space=pltpu.SMEM),
-            anywhere,
-            anywhere,
-            anywhere,
-            vmem,
-            vmem,
-            anywhere,
-        ],
-        out_specs=(anywhere, vmem),
+        out_shape=(pltpu.VMEM((tok, feat), BF16), pltpu.VMEM((rows, feat), F32)),
+        in_specs=[anywhere] * 7,
+        out_specs=(vmem, vmem),
         scratch_shapes=[
+            pltpu.VMEM(history.shape, BF16),
+            pltpu.VMEM(offsets.shape, jnp.int32),
+            pltpu.SMEM(frame_counts.shape, jnp.int32),
             pltpu.VMEM((NX, tok, HD), BF16),
             pltpu.VMEM((WINB - 1 + NX, tok, HD), BF16),
             pltpu.VMEM((WINB - 1 + NX, tok, HD), BF16),
@@ -495,7 +487,7 @@
             pltpu.VMEM((total_rows, feat), BF16),
             pltpu.VMEM((blocks, lines, 128), BF16),
             pltpu.VMEM((blocks, lines, 128), F32),
-            dma((6,)),
+            dma((8,)),
             dma((1,)),
             dma((1,)),
             dma((NX,)),
@@ -520,15 +512,6 @@
         offsets,
         cotangent,
     )
-    return pl.pallas_call(
-        hand_on,
-        out_shape=(
-            jax.ShapeDtypeStruct((tok, feat), BF16),
-            jax.ShapeDtypeStruct((rows, feat), F32),
-        ),
-        in_specs=[vmem, vmem],
-        out_specs=(vmem, vmem),
-    )(*results)
 
 
 def solution(mesh):

time: 61 us -> 59.3 us (0.972)
  Pallas kernels: 60.2 us -> 57.2 us
  local copies, waits for them, and re-layouts: 0 us -> 1.32 us
    pallas_call x1 -> x0, Pallas kernels: 1.68 us -> none  [body(): pl.pallas_call(hand_on, out_shape=(jax.ShapeDtypeStruct((tok, feat), BF16...]
    unnamed x0 -> x2, local copies, waits for them, and re-layouts: none -> 1.32 us
    pallas_call x1, Pallas kernels: 58.5 us -> 57.2 us  [body(): pl.pallas_call(make_kernel(blocks, tok, feat, tiles, outs, streams), out_...]
where the time goes in v4:
time: 59.3 us; the launch traced here: 59.2 us
  Pallas kernels  57.2 us (96%)
  local copies, waits for them, and re-layouts  1.32 us (2%)
  between operations  0.64 us (1%)
    pallas_call x1, Pallas kernels, body(): pl.pallas_call(make_kernel(blocks, tok, feat, tiles, outs, streams), out_...  57.2 us
    unnamed x2, local copies, waits for them, and re-layouts  1.32 us

profile of v4, /device:TPU:256, one launch (start us, length us, event | category | flops | bytes accessed | tf_op | source)
XLA Modules:
  0.0 59.2 jit_solution(8783844346740524107)
XLA Ops:
  0.6 57.2 %shard_map.86 = (bf16[256,512]{1,0:T(8,128)(2,1)S(1)}, f32[16,512]{1,0:T(8,128)S(1)}) custom-call(s32[128]{0:T(128)} %counts_hbm.1, bf16[256,512]{1,0:T(8,128)(2,1)} %query_hbm.1, bf16[256,512]{1,0:T(8,128)(2,1)} %key_hbm.1, bf16[256,512]{1,0:T(8,128)(2,1)} %value_hbm.1, bf16[2,512]{1,0:T(2,128)(2,1)} %history_hbm.1, s32[1,128]{1,0:T(1,128)} %offsets_hbm.1, ...), custom_call_target="tpu_custom_call" | custom-call | tf_op jit(solution)/shard_map/pallas_call | solution.py:472
  57.8 0.7 %copy.11 = bf16[256,512]{1,0:T(8,128)(2,1)} copy(bf16[256,512]{1,0:T(8,128)(2,1)S(1)} %get-tuple-element.2) | data formatting | bytes 524288
  58.5 0.6 %copy.12 = f32[16,512]{1,0:T(8,128)} copy(f32[16,512]{1,0:T(8,128)S(1)} %get-tuple-element.3) | data formatting | bytes 65536

commit v5 on v4

--- a/solution.py
+++ b/solution.py
@@ -46,7 +46,7 @@
         *stream_refs,
     ):
         me = lax.axis_index("tm")
-        refs = [stream_refs[18 * i : 18 * (i + 1)] for i in range(len(streams))]
+        refs = [stream_refs[14 * i : 14 * (i + 1)] for i in range(len(streams))]
         x = lax.rem(me, NX)
         y = lax.rem(me // NX, NY)
         z = me // (NX * NY)
@@ -108,7 +108,7 @@
                         kv_recv.at[which * (NX - 1) + k - 1],
                         at_x(k),
                     )
-                    for k in range(1, NX)
+                    for k in (2, 1, 3)
                 ]
             )
         ahead = [
@@ -302,7 +302,6 @@
             return copy
 
         stage2 = [[None] * 3 for _ in streams]
-        stage3 = [[None] * (nz - 1) for _ in streams]
         relays = [[None] * 4 for _ in streams]
         direct = [[[None] * 4 for _ in range(2)] for _ in streams]
 
@@ -317,19 +316,19 @@
         up, down = (1, 3), (2, 0)
 
         def opposite(i):
-            s0, r0 = refs[i][13], refs[i][14]
+            s0, r0 = refs[i][9], refs[i][10]
             s0[...] = dot1(i, 2).astype(BF16)
             for j in (1, 2, 3, 0):
                 relays[i][j] = send(
                     s0.at[j],
                     r0.at[j],
-                    refs[i][15].at[j],
-                    refs[i][16].at[j],
+                    refs[i][11].at[j],
+                    refs[i][12].at[j],
                     reach[streams[i]](1 if j in up else 3),
                 )
 
         def pass1(i, side, js):
-            s1, r1, s1_sem, r1_sem = refs[i][0], refs[i][1], refs[i][7], refs[i][8]
+            s1, r1, s1_sem, r1_sem = refs[i][0], refs[i][1], refs[i][5], refs[i][6]
             for j in js:
                 direct[i][side][j] = send(
                     s1.at[side, j],
@@ -344,7 +343,7 @@
             through = up if side == 0 else down
             for j in range(4):
                 if j in through:
-                    refs[i][17][j] = block[j]
+                    refs[i][13][j] = block[j]
                 else:
                     refs[i][0][side, j] = block[j].astype(BF16)
             pass1(i, side, down if side == 0 else up)
@@ -352,7 +351,7 @@
         def through1(i, side):
             for j in up if side == 0 else down:
                 relays[i][j].wait_recv()
-                total = refs[i][17][j] + refs[i][14][j].astype(F32)
+                total = refs[i][13][j] + refs[i][10][j].astype(F32)
                 refs[i][0][side, j] = total.astype(BF16)
                 pass1(i, side, (j,))
 
@@ -368,33 +367,31 @@
             stage2[i][j - 1] = send(
                 s2.at[j - 1],
                 r2.at[j - 1],
-                refs[i][9].at[j - 1],
-                refs[i][10].at[j - 1],
+                refs[i][7].at[j - 1],
+                refs[i][8].at[j - 1],
                 reach[1 - streams[i]](j),
             )
 
-        def third(i):
-            own1, r2, s3, r3 = refs[i][2], refs[i][4], refs[i][5], refs[i][6]
-            arrive(stage2[i])
-            total = own1[0]
-            for k in range(3):
-                total += r2[k].astype(F32)
-            own1[1, 0] = total[0]
-            s3[...] = total[1:].astype(BF16)
-            for k in range(1, nz):
-                stage3[i][k - 1] = send(
-                    s3.at[k - 1],
-                    r3.at[k - 1],
-                    refs[i][11].at[k - 1],
-                    refs[i][12].at[k - 1],
-                    at_z(k),
-                )
+        s3, r3, s3_sem, r3_sem = stream_refs[-4:]
+
+        def third():
+            for i in every:
+                own1, r2 = refs[i][2], refs[i][4]
+                arrive(stage2[i])
+                total = own1[0]
+                for k in range(3):
+                    total += r2[k].astype(F32)
+                own1[1, 0] = total[0]
+                s3[:, :, halves[i]] = total[1:].astype(BF16)
+            return [
+                send(s3.at[k], r3.at[k], s3_sem.at[k], r3_sem.at[k], at_z(k + 1))
+                for k in range(nz - 1)
+            ]
 
         def finish(i):
-            arrive(stage3[i])
             total = refs[i][2][1, 0]
             for k in range(nz - 1):
-                total += refs[i][6][k].astype(F32)
+                total += r3[k, :, halves[i]].astype(F32)
             grad_ref[:, halves[i]] = total
 
         every = range(len(streams))
@@ -415,8 +412,7 @@
         for j in (1, 2, 3, 0):
             for i in every:
                 second(i, j)
-        for i in every:
-            third(i)
+        stage3 = third()
         write_back.wait()
         pl.when(has_after)(forward.wait_send)
         for copy in ahead:
@@ -425,6 +421,7 @@
             pl.when(x != i)(backs[i].wait_send)
         for copy in swaps[0] + swaps[1] + swaps[2] + gather_x + gather_y + gather_z + sends:
             copy.wait_send()
+        arrive(stage3)
         for i in every:
             finish(i)
 
@@ -455,20 +452,22 @@
             pltpu.VMEM((4, nz, rows, width), F32),
             pltpu.VMEM((3, nz, rows, width), BF16),
             pltpu.VMEM((3, nz, rows, width), BF16),
-            pltpu.VMEM((nz - 1, rows, width), BF16),
-            pltpu.VMEM((nz - 1, rows, width), BF16),
             dma((2, 4)),
             dma((2, 4)),
             dma((3,)),
             dma((3,)),
-            dma((nz - 1,)),
-            dma((nz - 1,)),
             pltpu.VMEM((4, nz, rows, width), BF16),
             pltpu.VMEM((4, nz, rows, width), BF16),
             dma((4,)),
             dma((4,)),
             pltpu.VMEM((4, nz, rows, width), F32),
         ]
+    stream_scratch += [
+        pltpu.VMEM((nz - 1, rows, feat), BF16),
+        pltpu.VMEM((nz - 1, rows, feat), BF16),
+        dma((nz - 1,)),
+        dma((nz - 1,)),
+    ]
     return pl.pallas_call(
         make_kernel(blocks, tok, feat, tiles, outs, streams),
         out_shape=(pltpu.VMEM((tok, feat), BF16), pltpu.VMEM((rows, feat), F32)),

time: 59.3 us -> 58.9 us (level)
  no operation moved by 1% of the time
where the time goes in v5:
time: 58.9 us; the launch traced here: 58.8 us
  Pallas kernels  56.8 us (96%)
  local copies, waits for them, and re-layouts  1.32 us (2%)
  between operations  0.64 us (1%)
    pallas_call x1, Pallas kernels, body(): pl.pallas_call(make_kernel(blocks, tok, feat, tiles, outs, streams), out_...  56.8 us
    unnamed x2, local copies, waits for them, and re-layouts  1.32 us

profile of v5, /device:TPU:256, one launch (start us, length us, event | category | flops | bytes accessed | tf_op | source)
XLA Modules:
  0.0 58.8 jit_solution(1766134299568053155)
XLA Ops:
  0.6 56.8 %shard_map.86 = (bf16[256,512]{1,0:T(8,128)(2,1)S(1)}, f32[16,512]{1,0:T(8,128)S(1)}) custom-call(s32[128]{0:T(128)} %counts_hbm.1, bf16[256,512]{1,0:T(8,128)(2,1)} %query_hbm.1, bf16[256,512]{1,0:T(8,128)(2,1)} %key_hbm.1, bf16[256,512]{1,0:T(8,128)(2,1)} %value_hbm.1, bf16[2,512]{1,0:T(2,128)(2,1)} %history_hbm.1, s32[1,128]{1,0:T(1,128)} %offsets_hbm.1, ...), custom_call_target="tpu_custom_call" | custom-call | tf_op jit(solution)/shard_map/pallas_call | solution.py:471
  57.4 0.7 %copy.11 = bf16[256,512]{1,0:T(8,128)(2,1)} copy(bf16[256,512]{1,0:T(8,128)(2,1)S(1)} %get-tuple-element.2) | data formatting | bytes 524288
  58.1 0.6 %copy.12 = f32[16,512]{1,0:T(8,128)} copy(f32[16,512]{1,0:T(8,128)S(1)} %get-tuple-element.3) | data formatting | bytes 65536

commit v6 on v5

--- a/solution.py
+++ b/solution.py
@@ -108,7 +108,7 @@
                         kv_recv.at[which * (NX - 1) + k - 1],
                         at_x(k),
                     )
-                    for k in (2, 1, 3)
+                    for k in range(1, NX)
                 ]
             )
         ahead = [

time: 58.9 us -> 58.6 us (level)
  no operation moved by 1% of the time
where the time goes in v6:
time: 58.6 us; the launch traced here: 58.4 us
  Pallas kernels  56.5 us (96%)
  local copies, waits for them, and re-layouts  1.32 us (2%)
  between operations  0.64 us (1%)
    pallas_call x1, Pallas kernels, body(): pl.pallas_call(make_kernel(blocks, tok, feat, tiles, outs, streams), out_...  56.5 us
    unnamed x2, local copies, waits for them, and re-layouts  1.32 us

profile of v6, /device:TPU:256, one launch (start us, length us, event | category | flops | bytes accessed | tf_op | source)
XLA Modules:
  0.0 58.4 jit_solution(433198417408437753)
XLA Ops:
  0.6 56.5 %shard_map.86 = (bf16[256,512]{1,0:T(8,128)(2,1)S(1)}, f32[16,512]{1,0:T(8,128)S(1)}) custom-call(s32[128]{0:T(128)} %counts_hbm.1, bf16[256,512]{1,0:T(8,128)(2,1)} %query_hbm.1, bf16[256,512]{1,0:T(8,128)(2,1)} %key_hbm.1, bf16[256,512]{1,0:T(8,128)(2,1)} %value_hbm.1, bf16[2,512]{1,0:T(2,128)(2,1)} %history_hbm.1, s32[1,128]{1,0:T(1,128)} %offsets_hbm.1, ...), custom_call_target="tpu_custom_call" | custom-call | tf_op jit(solution)/shard_map/pallas_call | solution.py:471
  57.1 0.7 %copy.11 = bf16[256,512]{1,0:T(8,128)(2,1)} copy(bf16[256,512]{1,0:T(8,128)(2,1)S(1)} %get-tuple-element.2) | data formatting | bytes 524288
  57.8 0.6 %copy.12 = f32[16,512]{1,0:T(8,128)} copy(f32[16,512]{1,0:T(8,128)S(1)} %get-tuple-element.3) | data formatting | bytes 65536
